TPU v7x, 32 devices: a whole 2x2x4 slice. The times are simulated.
32 devices in a mesh: grp: 2 (over y), lat: 4 (over z), chan: 2 (over core), ens: 2 (over x).
Axes of the slice: x: 2, y: 2, z: 4, core: 2. Of those that a mesh axis runs over, the one named last changes fastest.
Arguments:
- grad_out: bfloat16 [4, 24, 48, 384], P(('grp', 'ens'), 'lat', None, 'chan'), parts along dimension 0, may hold values from -6 to 6
- pre_act: bfloat16 [4, 24, 48, 384], P(('grp', 'ens'), 'lat', None, 'chan'), parts along dimension 0, may hold values from -6 to 6
- coeffs: bfloat16 [4, 24, 24, 2, 384], P(('grp', 'ens'), ('lat', 'chan')), parts along dimension 0, may hold values from -6 to 6
- legendre: bfloat16 [24, 24, 24], P(('lat', 'chan'), None, 'ens'), may hold values from -1.25 to 1.25
- mixing: bfloat16 [384, 384], replicated, may hold values from -0.3125 to 0.3125
Outputs:
- grad_in: bfloat16 [4, 24, 48, 384], P(('grp', 'ens'), 'lat', None, 'chan'), parts along dimension 0
- mixing_grad: float32 [768, 384], P('grp'), parts along dimension 0
There are 2 independent parts, one for each index of `grp`. A program takes and returns all parts, laid end to end along the dimension named above; an argument that names none is the same for every part. Nothing has to cross between parts.
All inputs are finite; a program needn't handle non-finite values.
Results may differ from a plain program's by a relative error of at most 0.0074.
Values may be sent and summed in bfloat16 or wider, within the bound.
A program may use at most 64 MiB of HBM per device.

v0:
```python
import math

import jax
import jax.numpy as jnp
from jax import lax
from jax.sharding import PartitionSpec as P


def fourier_table(lon_count, mode_count):
    longitude = jnp.arange(lon_count, dtype=jnp.int32)[:, None]
    wavenumber = jnp.arange(mode_count, dtype=jnp.int32)[None, :]
    product_index = longitude * wavenumber % lon_count
    angles = 2.0 * math.pi / lon_count * product_index.astype(jnp.float32)
    factor = math.sqrt(2.0 / lon_count)
    stacked = jnp.stack([jnp.cos(angles), -jnp.sin(angles)], axis=2) * factor
    return stacked.reshape(lon_count, 2 * mode_count).astype(jnp.bfloat16)


def silu_backward(cotangent, preact):
    values = preact.astype(jnp.float32)
    gate_value = jax.nn.sigmoid(values)
    return (
        cotangent.astype(jnp.float32) * gate_value * (1.0 + values * (1.0 - gate_value))
    ).astype(jnp.bfloat16)


def on_device(grad_out, pre_act, coeffs, legendre, mixing):
    lat_rows = grad_out.shape[1]
    lon_count = grad_out.shape[2]
    chan_cols = grad_out.shape[3]
    mode_count = lon_count // 2
    lat_devices = lax.axis_size("lat")
    chan_count = lax.axis_size("chan")
    members = lax.axis_size("ens")
    lat_count = lat_rows * lat_devices
    channels = chan_cols * chan_count
    mode_width = 2 * mode_count // (lat_devices * chan_count)
    local_modes = mode_width // 2
    fourier = fourier_table(lon_count, mode_count)
    scaled = silu_backward(grad_out[0], pre_act[0])
    spectral = jnp.einsum(
        "nk,anc->akc", fourier, scaled, preferred_element_type=jnp.float32
    ).astype(jnp.bfloat16)
    exchanged = lax.all_to_all(
        lax.all_to_all(spectral, "lat", split_axis=1, concat_axis=0, tiled=True),
        "chan",
        split_axis=1,
        concat_axis=2,
        tiled=True,
    )
    spectral_modes = exchanged.reshape(lat_count, local_modes, 2, channels)
    legendre_full = lax.all_gather(legendre, "ens", axis=2, tiled=True)
    coef_grad = jnp.einsum(
        "mla,amrc->mlrc", legendre_full, spectral_modes, preferred_element_type=jnp.float32
    ).astype(jnp.bfloat16)
    stored = coeffs[0].reshape(-1, channels)
    flat_grad = coef_grad.reshape(-1, channels)
    weight_grad = lax.dot_general(
        stored, flat_grad, (((0,), (0,)), ((), ())), preferred_element_type=jnp.float32
    )
    weight_grad = weight_grad * (1.0 / (members * mode_count))
    weight_grad = lax.psum(weight_grad, ("lat", "chan", "ens"))
    mixed_grad = lax.dot_general(
        coef_grad, mixing, (((3,), (1,)), ((), ())), preferred_element_type=jnp.float32
    ).astype(jnp.bfloat16)
    returned = jnp.einsum(
        "mla,mlrc->amrc", legendre_full, mixed_grad, preferred_element_type=jnp.float32
    ).astype(jnp.bfloat16)
    shaped = returned.reshape(lat_count, 1, mode_width, channels)
    received = lax.all_to_all(
        lax.all_to_all(shaped, "lat", split_axis=0, concat_axis=1, tiled=True),
        "chan",
        split_axis=3,
        concat_axis=2,
        tiled=True,
    )
    row_coeffs = received.reshape(lat_rows, 2 * mode_count, chan_cols)
    spatial = jnp.einsum("nk,akc->anc", fourier, row_coeffs, preferred_element_type=jnp.float32)
    result = (grad_out[0].astype(jnp.float32) + spatial).astype(jnp.bfloat16)
    return (result[None], weight_grad)


def solution(mesh):
    placed = (
        P(("grp", "ens"), "lat", None, "chan"),
        P(("grp", "ens"), "lat", None, "chan"),
        P(("grp", "ens"), ("lat", "chan"), None, None, None),
        P(("lat", "chan"), None, "ens"),
        P(),
    )
    return jax.shard_map(
        on_device,
        mesh=mesh,
        in_specs=placed,
        out_specs=(P(("grp", "ens"), "lat", None, "chan"), P("grp", None)),
        check_vma=False,
    )
```

profile of v0, /device:TPU:0, one launch (start us, length us, event | category | flops | bytes accessed | tf_op | source)
XLA Modules:
  0.0 128.6 jit_solution(154595205387489412)
XLA Ops:
  7.2 0.0 copy-start
  7.2 0.0 copy-start.3
  7.2 0.0 copy-start.2
  7.2 0.1 sine_negate_fusion
  7.3 1.3 fusion.4
  8.6 0.7 copy.47
  9.3 6.3 %all-to-all-start = ((bf16[6,48,192]{2,0,1:T(8,128)(2,1)}), bf16[6,48,192]{2,0,1:T(8,128)(2,1)S(1)}, u32[]{:S(2)}, u32[]{:S(2)}) async-start(bf16[6,48,192]{2,0,1:T(8,128)(2,1)} %copy.47), calls=%async_computation | async-start | bytes 393216 | tf_op jit(solution)/shard_map/all_to_all | solution.py:45
  15.6 0.0 all-reduce.2.cloned.1.call-start
  15.6 0.0 copy-done.3
  15.6 0.0 copy-done.2
  15.7 4.4 %all_gather.3 = bf16[3,24,24]{1,0,2:T(4,128)(2,1)S(1)} all-gather(bf16[3,24,12]{1,0,2:T(4,128)(2,1)S(1)} %copy.51), channel_id=1, replica_groups=mesh['grp'=2,'lat'=4,'chan'=2,'ens'=2] {'ens'}, dimensions={2}, use_global_device_ids=true | all-gather | bytes 5184 | tf_op jit(solution)/shard_map/all_gather | solution.py:52
  20.1 3.0 %all-to-all-done = bf16[6,48,192]{2,0,1:T(8,128)(2,1)S(1)} async-done(((bf16[6,48,192]{2,0,1:T(8,128)(2,1)}), bf16[6,48,192]{2,0,1:T(8,128)(2,1)S(1)}, u32[]{:S(2)}, u32[]{:S(2)}) %all-to-all-start) | async-done | bytes 110624 | tf_op jit(solution)/shard_map/all_to_all | solution.py:45
  23.2 0.1 all_to_all.51
  23.3 3.8 %all_to_all.66 = bf16[24,12,192]{2,0,1:T(8,128)(2,1)S(1)} all-to-all(bf16[24,12,192]{2,0,1:T(8,128)(2,1)S(1)} %all_to_all.51), channel_id=1, replica_groups=mesh['grp'=2,'lat'=4,'chan'=2,'ens'=2] {'chan'}, dimensions={1} | all-to-all | bytes 221184 | tf_op jit(solution)/shard_map/all_to_all | solution.py:44
  27.1 0.1 copy.50
  27.2 0.1 reshape.90
  27.3 0.2 fusion.5
  27.6 0.1 copy.60
  27.7 1.1 fusion
  28.8 0.0 all-reduce.2.cloned.1.call-update
  28.9 0.0 copy-done
  28.9 0.4 convolution_convert_fusion.1
  29.3 9.9 %all_to_all.67 = bf16[24,1,6,384]{3,2,1,0:T(8,128)(2,1)S(1)} all-to-all(bf16[24,1,6,384]{3,2,1,0:T(8,128)(2,1)S(1)} %copy.54), channel_id=1, replica_groups=mesh['grp'=2,'lat'=4,'chan'=2,'ens'=2] {'lat'}, dimensions={0} | all-to-all | bytes 221184 | tf_op jit(solution)/shard_map/all_to_all | solution.py:71
  39.3 1.5 %copy.56 = bf16[6,4,6,384]{0,1,2,3:T(4,128)(2,1)S(1)} copy(bf16[6,4,6,384]{3,2,0,1:T(8,128)(2,1)S(1)} %bitcast.68) | data formatting | bytes 221184 | tf_op jit(solution)/shard_map/all_to_all | solution.py:71
  40.7 4.1 %reshape.100 = bf16[2,2,13824]{2,1,0:T(2,128)(2,1)S(1)} reshape(bf16[384,6,4,6]{3,2,1,0:T(4,128)(2,1)S(1)} %bitcast.65) | data formatting | bytes 221184
  44.8 3.8 %all_to_all.68 = bf16[2,2,13824]{2,1,0:T(2,128)(2,1)S(1)} all-to-all(bf16[2,2,13824]{2,1,0:T(2,128)(2,1)S(1)} %reshape.100), channel_id=1, replica_groups=mesh['grp'=2,'lat'=4,'chan'=2,'ens'=2] {'chan'}, dimensions={0} | all-to-all | bytes 221184 | tf_op jit(solution)/shard_map/all_to_all | solution.py:70
  48.7 5.4 %reshape.101 = bf16[384,6,4,6]{3,2,1,0:T(4,128)(2,1)S(1)} reshape(bf16[2,2,13824]{2,1,0:T(2,128)(2,1)S(1)} %all_to_all.68) | data formatting | bytes 221184
  54.0 2.5 %copy.74 = bf16[6,4,6,2,192]{4,3,1,2,0:T(2,128)(2,1)S(1)} copy(bf16[6,4,6,2,192]{0,1,2,4,3:T(4,128)(2,1)S(1)} %bitcast.66) | data formatting | bytes 221184 | tf_op jit(solution)/shard_map/all_to_all | solution.py:70
  56.6 0.1 reshape.92
  56.7 0.9 fusion.3
  57.6 62.1 %all-reduce.2.cloned.1.call-done = f32[384,384]{0,1:T(8,128)} async-done(((f32[384,384]{0,1:T(8,128)}), f32[384,384]{0,1:T(8,128)}) %all-reduce.2.cloned.1.call-update) | async-done | bytes 589840 | tf_op jit(solution)/shard_map/psum | solution.py:62
  119.7 2.1 %copy.61 = f32[384,384]{1,0:T(8,128)} copy(f32[384,384]{0,1:T(8,128)} %all-reduce.2.cloned.1.call-done) | data formatting | bytes 1179648
  (10 shorter events, 0.2 us)
Async XLA Ops:
  7.2 21.7 %copy-start = (bf16[384,384]{1,0:T(8,128)(2,1)S(1)}, bf16[384,384]{1,0:T(8,128)(2,1)}, u32[]{:S(2)}) copy-start(bf16[384,384]{1,0:T(8,128)(2,1)} %param.9) | copy-start | bytes 884740
  7.2 8.4 %copy-start.3 = (bf16[3,24,12]{1,2,0:T(8,128)(2,1)S(1)}, bf16[3,24,12]{1,2,0:T(8,128)(2,1)}, u32[]{:S(2)}) copy-start(bf16[3,24,12]{1,2,0:T(8,128)(2,1)} %param.8) | copy-start | bytes 5188
  7.2 8.4 %copy-start.2 = (bf16[1,3,24,2,384]{4,3,2,1,0:T(2,128)(2,1)S(1)}, bf16[1,3,24,2,384]{4,3,2,1,0:T(2,128)(2,1)}, u32[]{:S(2)}) copy-start(bf16[1,3,24,2,384]{4,3,2,1,0:T(2,128)(2,1)} %param.7) | copy-start | bytes 331780
  9.3 13.8 %all-to-all-start = ((bf16[6,48,192]{2,0,1:T(8,128)(2,1)}), bf16[6,48,192]{2,0,1:T(8,128)(2,1)S(1)}, u32[]{:S(2)}, u32[]{:S(2)}) async-start(bf16[6,48,192]{2,0,1:T(8,128)(2,1)} %copy.47), calls=%async_computation | async-start | bytes 393216 | tf_op jit(solution)/shard_map/all_to_all | solution.py:45
  15.6 104.0 %all-reduce.2.cloned.1.call-start = ((), (), s32[]{:S(2)}) async-start(), calls=%async_computation.4 | async-start | bytes 1179648 | tf_op jit(solution)/shard_map/psum | solution.py:62
  48.7 8.0 %copy-start.1 = (bf16[1,6,48,192]{3,2,1,0:T(8,128)(2,1)S(1)}, bf16[1,6,48,192]{3,2,1,0:T(8,128)(2,1)}, u32[]{:S(2)}) copy-start(bf16[1,6,48,192]{3,2,1,0:T(8,128)(2,1)} %param.5) | copy-start | bytes 331780
Sparse Core Ops, SparseCore 0:
  29.0 90.6 all-reduce.1
where the time goes:
time: 129 us
  waiting for transfers between devices  65.2 us (51%)
  blocking collectives  22 us (17%)
  local copies, waits for them, and re-layouts  17 us (13%)
  between operations  14.2 us (11%)
  starting transfers between devices  6.32 us (5%)
  matrix products  3.94 us (3%)
    psum x1, waiting for transfers between devices, on_device(): weight_grad = lax.psum(weight_grad, ('lat', 'chan', 'ens'))  62.1 us
    unnamed x12, local copies, waits for them, and re-layouts  11.6 us
    all_to_all x1, blocking collectives, on_device(): lax.all_to_all(shaped, 'lat', split_axis=0, concat_axis=1, tiled=True)  9.92 us
    all_to_all x1, starting transfers between devices, on_device(): lax.all_to_all(spectral, 'lat', split_axis=1, concat_axis=0, tiled=True)  6.32 us
    all_gather x1, blocking collectives, on_device(): legendre_full = lax.all_gather(legendre, 'ens', axis=2, tiled=True)  4.4 us
    all_to_all x1, blocking collectives, on_device(): lax.all_to_all(lax.all_to_all(spectral, 'lat', split_axis=1, concat_axis=...  3.82 us
    all_to_all x1, blocking collectives, on_device(): lax.all_to_all(lax.all_to_all(shaped, 'lat', split_axis=0, concat_axis=1,...  3.81 us
    all_to_all x1, waiting for transfers between devices, on_device(): lax.all_to_all(spectral, 'lat', split_axis=1, concat_axis=0, tiled=True)  3.04 us
  transfers between devices with their start and end apart: 2, of which 2 were waited for; matrix products, arithmetic and copies ran while one was open for 12% of the time, Pallas kernels for 0%

commit v1 on v0

--- a/solution.py
+++ b/solution.py
@@ -2,7 +2,10 @@
 
 import jax
 import jax.numpy as jnp
+import numpy as np
 from jax import lax
+from jax.experimental import pallas as pl
+from jax.experimental.pallas import tpu as pltpu
 from jax.sharding import PartitionSpec as P
 
 
@@ -79,6 +82,263 @@
     result = (grad_out[0].astype(jnp.float32) + spatial).astype(jnp.bfloat16)
     return (result[None], weight_grad)
 
+MESH = pl.DeviceIdType.MESH
+BF16 = jnp.bfloat16
+F32 = jnp.float32
+
+
+def dot(a, b, dims=((1,), (0,))):
+    return lax.dot_general(a, b, (dims, ((), ())), preferred_element_type=F32)
+
+
+def tables(rows, lon, lats, chans, members, modes, degrees):
+    owners = lats * chans
+    width = 2 * modes
+    pad = -(-rows * width // 16) * 16
+    n = np.arange(lon)[:, None]
+    m = np.arange(lon // 2)[None, :]
+    angles = np.float32(2.0 * math.pi / lon) * (n * m % lon).astype(np.float32)
+    table = np.stack([np.cos(angles), -np.sin(angles)], axis=2).reshape(lon, lon)
+    table = (table * np.float32(math.sqrt(2.0 / lon))).astype(np.float32)
+    inverse = np.zeros((rows, lon, owners, pad), np.float32)
+    for a in range(rows):
+        for d in range(owners):
+            inverse[a, :, d, a * width:(a + 1) * width] = table[:, d * width:(d + 1) * width]
+    inverse = inverse.reshape(rows * lon, owners * pad)
+    lat_of = np.full((lats, pad), -1)
+    key_of = np.full((lats, pad), -1)
+    for z in range(lats):
+        for a in range(rows):
+            for k in range(width):
+                lat_of[z, a * width + k] = z * rows + a
+                key_of[z, a * width + k] = k
+    lat_of, key_of = lat_of.reshape(-1), key_of.reshape(-1)
+    held = rows * lats // members
+    select = (lat_of[None, :] == np.arange(members * held)[:, None]).astype(np.float32)
+    select = select.reshape(members, held, -1)
+    row = np.arange(modes * degrees * 2)
+    spread = (row[:, None] // 2 == np.arange(modes * degrees)[None, :]).astype(np.float32)
+    row_key = row // (2 * degrees) * 2 + row % 2
+    mask = (row_key[:, None] == key_of[None, :]).astype(np.float32)
+    cast = lambda x: jnp.asarray(np.ascontiguousarray(x), BF16)
+    return (
+        cast(inverse.T), cast(inverse), cast(select), cast(select.transpose(0, 2, 1)),
+        cast(spread), cast(spread.T), cast(mask), cast(mask.T),
+    )
+
+
+def fused_kernel(
+    lats, chans, members,
+    grad_ref, pre_ref, coeffs_ref, leg_ref, mix_ref,
+    fwd_ref, inv_ref, sel_ref, selt_ref, spread_ref, spreadt_ref, mask_ref, maskt_ref,
+    out_ref, full_ref,
+    lbuf, sbuf, rbuf, sbuf2, rbuf2, wown, w1s, w1r, w2own, w2s, w2r,
+    lsem, esem, fsem, r1sem, r2sem, g1sem, g2sem,
+):
+    z, c, x = lax.axis_index("lat"), lax.axis_index("chan"), lax.axis_index("ens")
+    owners, quads = lats * chans, members * chans
+    me, quad = z * chans + c, x * chans + c
+    pad, cols = rbuf.shape[2], rbuf.shape[3]
+
+    def owner_peer(p):
+        q = lax.rem(me + p, owners)
+        return q, q // chans, lax.rem(q, chans)
+
+    def quad_peer(p):
+        q = lax.rem(quad + p, quads)
+        return q, q // chans, lax.rem(q, chans)
+
+    barrier = pltpu.get_barrier_semaphore()
+    for p in range(1, owners):
+        _, pz, pc = owner_peer(p)
+        pl.semaphore_signal(barrier, inc=1, device_id={"lat": pz, "chan": pc}, device_id_type=MESH)
+    for p in range(1, members):
+        for pc in range(chans):
+            target = {"ens": lax.rem(x + p, members), "chan": pc}
+            pl.semaphore_signal(barrier, inc=1, device_id=target, device_id_type=MESH)
+
+    values = pre_ref[...].astype(F32)
+    gate = jax.nn.sigmoid(values)
+    scaled = (grad_ref[...].astype(F32) * gate * (1.0 + values * (1.0 - gate))).astype(BF16)
+    sbuf[...] = dot(fwd_ref[...], scaled).astype(BF16).reshape(owners, pad, cols)
+
+    pl.semaphore_wait(barrier, owners - 1 + (members - 1) * chans)
+
+    def remote(src, dst, sems, target):
+        return pltpu.make_async_remote_copy(
+            src_ref=src, dst_ref=dst, send_sem=sems[0], recv_sem=sems[1],
+            device_id=target, device_id_type=MESH,
+        )
+
+    def pair(sem, *index):
+        return sem.at[(0,) + index], sem.at[(1,) + index]
+
+    started = []
+    first = []
+    for p in range(1, owners):
+        q, pz, pc = owner_peer(p)
+        copy = remote(sbuf.at[q], rbuf.at[c, z], pair(esem, p - 1), {"lat": pz, "chan": pc})
+        copy.start()
+        first.append(copy)
+    legs = remote(leg_ref, lbuf, pair(lsem, 0), {"ens": lax.rem(x + 1, members)})
+    legs.start()
+    started += first + [legs]
+    rbuf[c, z] = sbuf[me]
+    legs.wait_recv()
+    other = lax.rem(x + 1, members)
+    mine, theirs = leg_ref[...], lbuf[...]
+    by_lat = dot(mine, sel_ref[x]) + dot(theirs, sel_ref[other])
+    analysis = (dot(spread_ref[...], by_lat.astype(BF16)) * mask_ref[...].astype(F32)).astype(BF16)
+    across = ((1,), (1,))
+    by_row = dot(selt_ref[x], mine, across) + dot(selt_ref[other], theirs, across)
+    synthesis = (dot(by_row.astype(BF16), spreadt_ref[...]) * maskt_ref[...].astype(F32)).astype(BF16)
+
+    for copy in first:
+        copy.wait_recv()
+    halves = [dot(analysis, rbuf[h].reshape(lats * pad, cols)) for h in range(chans)]
+    coef = jnp.concatenate(halves, axis=1).astype(BF16)
+
+    weight = dot(coeffs_ref[...], coef, ((0,), (0,))).reshape(w1s.shape)
+    wown[...] = weight
+    w1s[...] = weight.astype(BF16)
+    reduce1 = []
+    for p in range(1, quads):
+        q, px, pc = quad_peer(p)
+        copy = remote(w1s.at[q], w1r.at[p - 1], pair(r1sem, p - 1), {"ens": px, "chan": pc})
+        copy.start()
+        reduce1.append(copy)
+    started += reduce1
+
+    for h in range(chans):
+        mixed = dot(coef, mix_ref[h * cols:(h + 1) * cols, :], across).astype(BF16)
+        sbuf2[h] = dot(synthesis, mixed).astype(BF16).reshape(lats, pad, cols)
+    second = []
+    for p in range(1, owners):
+        q, pz, pc = owner_peer(p)
+        copy = remote(sbuf2.at[pc, pz], rbuf2.at[me], pair(fsem, p - 1), {"lat": pz, "chan": pc})
+        copy.start()
+        second.append(copy)
+    started += second
+    rbuf2[me] = sbuf2[c, z]
+
+    total = wown[quad]
+    for p, copy in enumerate(reduce1):
+        copy.wait_recv()
+        total = total + w1r[p].astype(F32)
+    total = total.reshape(w2own.shape)
+    w2own[...] = total
+    w2s[...] = total.astype(BF16)
+    reduce2 = []
+    for p in range(1, lats):
+        pz = lax.rem(z + p, lats)
+        copy = remote(w2s.at[pz], w2r.at[p - 1], pair(r2sem, p - 1), {"lat": pz})
+        copy.start()
+        reduce2.append(copy)
+    started += reduce2
+
+    for copy in second:
+        copy.wait_recv()
+    spatial = dot(inv_ref[...], rbuf2[...].reshape(owners * pad, cols))
+    out_ref[...] = (grad_ref[...].astype(F32) + spatial).astype(BF16)
+
+    piece = w2own[z]
+    for p, copy in enumerate(reduce2):
+        copy.wait_recv()
+        piece = piece + w2r[p].astype(F32)
+    full_ref[quad, z] = piece.astype(BF16)
+    gather1 = []
+    for p in range(1, lats):
+        pz = lax.rem(z + p, lats)
+        copy = remote(full_ref.at[quad, z], full_ref.at[quad, z], pair(g1sem, p - 1), {"lat": pz})
+        copy.start()
+        gather1.append(copy)
+    started += gather1
+    gather2 = []
+    for s in range(lats):
+        if s > 0:
+            gather1[s - 1].wait_recv()
+        source = lax.rem(z + lats - s, lats)
+        for p in range(1, quads):
+            q, px, pc = quad_peer(p)
+            block = full_ref.at[quad, source]
+            copy = remote(block, block, pair(g2sem, p - 1, s), {"ens": px, "chan": pc})
+            copy.start()
+            gather2.append(copy)
+    for copy in gather2:
+        copy.wait_recv()
+    started += gather2
+    for copy in started:
+        copy.wait_send()
+
+
+def fused(grad_out, pre_act, coeffs, legendre, mixing):
+    rows, lon, cols = grad_out.shape[1:]
+    lats, chans = lax.axis_size("lat"), lax.axis_size("chan")
+    members = lax.axis_size("ens")
+    modes, degrees, held = legendre.shape
+    owners, quads, channels = lats * chans, members * chans, cols * chans
+    pad = -(-rows * 2 * modes // 16) * 16
+    part, piece = channels // quads, channels // quads // lats
+    constants = tables(rows, lon, lats, chans, members, modes, degrees)
+    dma = pltpu.SemaphoreType.DMA
+    vmem = pl.BlockSpec(memory_space=pltpu.VMEM)
+
+    def kernel(*refs):
+        fused_kernel(lats, chans, members, *refs)
+
+    result, weight = pl.pallas_call(
+        kernel,
+        out_shape=(
+            jax.ShapeDtypeStruct((rows * lon, cols), BF16),
+            jax.ShapeDtypeStruct((quads, lats, piece, channels), BF16),
+        ),
+        in_specs=[vmem] * 13,
+        out_specs=(vmem, vmem),
+        scratch_shapes=[
+            pltpu.VMEM((modes * degrees, held), BF16),
+            pltpu.VMEM((owners, pad, cols), BF16),
+            pltpu.VMEM((chans, lats, pad, cols), BF16),
+            pltpu.VMEM((chans, lats, pad, cols), BF16),
+            pltpu.VMEM((owners, pad, cols), BF16),
+            pltpu.VMEM((quads, part, channels), F32),
+            pltpu.VMEM((quads, part, channels), BF16),
+            pltpu.VMEM((quads - 1, part, channels), BF16),
+            pltpu.VMEM((lats, piece, channels), F32),
+            pltpu.VMEM((lats, piece, channels), BF16),
+            pltpu.VMEM((lats - 1, piece, channels), BF16),
+            dma((2, 1)),
+            dma((2, owners - 1)),
+            dma((2, owners - 1)),
+            dma((2, quads - 1)),
+            dma((2, lats - 1)),
+            dma((2, lats - 1)),
+            dma((2, quads - 1, lats)),
+        ],
+        compiler_params=pltpu.CompilerParams(
+            collective_id=0, has_side_effects=True, vmem_limit_bytes=32 << 20
+        ),
+    )(
+        grad_out.reshape(rows * lon, cols),
+        pre_act.reshape(rows * lon, cols),
+        coeffs.reshape(modes * degrees * 2, channels),
+        legendre.reshape(modes * degrees, held),
+        mixing,
+        *constants,
+    )
+    scale = 1.0 / (members * lon // 2)
+    return (
+        result.reshape(grad_out.shape),
+        weight.astype(F32).reshape(channels, channels) * scale,
+    )
+
+
+def fits(mesh, rows, lon, channels):
+    lats, chans, members = (mesh.shape[axis] for axis in ("lat", "chan", "ens"))
+    return (
+        members == 2 and lats * chans <= 8 and rows * lon <= 512
+        and lon % 16 == 0 and channels % (members * chans * lats * 8) == 0
+    )
+
 
 def solution(mesh):
     placed = (
@@ -88,8 +348,14 @@
         P(("lat", "chan"), None, "ens"),
         P(),
     )
+
+    def local(grad_out, *rest):
+        rows, lon, cols = grad_out.shape[1:]
+        small = fits(mesh, rows, lon, cols * mesh.shape["chan"])
+        return (fused if small else on_device)(grad_out, *rest)
+
     return jax.shard_map(
-        on_device,
+        local,
         mesh=mesh,
         in_specs=placed,
         out_specs=(P(("grp", "ens"), "lat", None, "chan"), P("grp", None)),

time: 129 us -> 40.3 us (0.31)
  waiting for transfers between devices: 65.2 us -> 0 us
  Pallas kernels: 0 us -> 27.9 us
  blocking collectives: 22 us -> 0 us
  between operations: 14.2 us -> 0.69 us
  local copies, waits for them, and re-layouts: 17 us -> 10.4 us
  starting transfers between devices: 6.32 us -> 0 us
  matrix products: 3.94 us -> 0 us
    psum x1 -> x0, waiting for transfers between devices: 62.1 us -> none  [on_device(): weight_grad = lax.psum(weight_grad, ('lat', 'chan', 'ens'))]
    pallas_call x0 -> x1, Pallas kernels: none -> 27.9 us  [fused(): pl.pallas_call(kernel, out_shape=(jax.ShapeDtypeStruct((rows * lon, cols)...]
    all_to_all x3 -> x0, blocking collectives: 17.6 us -> none  [the longest x1 9.92 us: on_device(): lax.all_to_all(shaped, 'lat', split_axis=0, concat_axis=1, tiled=True)]
    all_to_all x1 -> x0, starting transfers between devices: 6.32 us -> none  [on_device(): lax.all_to_all(spectral, 'lat', split_axis=1, concat_axis=0, tiled=True)]
    all_gather x1 -> x0, blocking collectives: 4.4 us -> none  [on_device(): legendre_full = lax.all_gather(legendre, 'ens', axis=2, tiled=True)]
    all_to_all x6 -> x0, local copies, waits for them, and re-layouts: 4.18 us -> none  [the longest x2 2.5 us: on_device(): lax.all_to_all(lax.all_to_all(shaped, 'lat', split_axis=0, concat_axis=1,...]
    dot_general x5 -> x0, matrix products: 3.94 us -> none  [the longest x1 1.26 us: on_device(): jnp.einsum('nk,anc->akc', fourier, scaled, preferred_element_type=jnp.flo...]
    all_to_all x1 -> x0, waiting for transfers between devices: 3.04 us -> none  [on_device(): lax.all_to_all(spectral, 'lat', split_axis=1, concat_axis=0, tiled=True)]
  transfers between devices with their start and end apart: 2 -> 0, of which waited for: 2 -> 0; matrix products, arithmetic and copies ran while one was open for 12% -> 0% of each run, Pallas kernels for 0% -> 0%
where the time goes in v1:
time: 40.3 us; the launch traced here: 39.8 us
  Pallas kernels  27.9 us (69%)
  local copies, waits for them, and re-layouts  10.4 us (26%)
  other arithmetic  0.87 us (2%)
  between operations  0.69 us (2%)
    pallas_call x1, Pallas kernels, fused(): pl.pallas_call(kernel, out_shape=(jax.ShapeDtypeStruct((rows * lon, cols)...  27.9 us
    unnamed x24, local copies, waits for them, and re-layouts  9.41 us
    reshape x1, local copies, waits for them, and re-layouts, fused(): coeffs.reshape(modes * degrees * 2, channels)  0.95 us
    mul x1, other arithmetic, fused(): weight.astype(F32).reshape(channels, channels) * scale  0.87 us

profile of v1, /device:TPU:0, one launch (start us, length us, event | category | flops | bytes accessed | tf_op | source)
XLA Modules:
  0.0 39.8 jit_solution(11104458727930638322)
XLA Ops:
  0.6 0.0 copy-start.2
  0.6 0.8 %copy.15 = bf16[3,24,12]{2,1,0:T(8,128)(2,1)S(1)} copy(bf16[3,24,12]{1,2,0:T(8,128)(2,1)} %param.16) | data formatting | bytes 3456 | tf_op args[3]
  1.5 0.0 copy-start.8
  1.5 0.9 %reshape.24.refs_2_ = bf16[144,384]{1,0:T(8,128)(2,1)S(1)} reshape(bf16[1,3,24,2,384]{4,3,2,1,0:T(2,128)(2,1)} %param.15) | data formatting | bytes 221184 | tf_op jit(solution)/shard_map/reshape | solution.py:323
  2.5 0.0 copy-done.2
  2.5 0.0 copy-done.8
  2.5 0.0 copy-start
  2.5 1.0 %copy-done = bf16[384,384]{1,0:T(8,128)(2,1)S(1)} copy-done((bf16[384,384]{1,0:T(8,128)(2,1)S(1)}, bf16[384,384]{1,0:T(8,128)(2,1)}, u32[]{:S(2)}) %copy-start) | copy-done | bytes 294936
  3.4 0.0 copy-start.1
  3.4 1.0 %copy-done.1 = bf16[384,288]{1,0:T(8,128)(2,1)S(1)} copy-done((bf16[384,288]{1,0:T(8,128)(2,1)S(1)}, bf16[384,288]{1,0:T(8,128)(2,1)}, u32[]{:S(2)}) %copy-start.1) | copy-done | bytes 221208
  4.4 0.0 copy-start.3
  4.4 0.9 %copy-done.3 = bf16[1,6,48,192]{3,2,1,0:T(8,128)(2,1)S(1)} copy-done((bf16[1,6,48,192]{3,2,1,0:T(8,128)(2,1)S(1)}, bf16[1,6,48,192]{3,2,1,0:T(8,128)(2,1)}, u32[]{:S(2)}) %copy-start.3) | copy-done | bytes 110616
  5.3 0.0 copy-start.4
  5.3 0.9 %copy-done.4 = bf16[1,6,48,192]{3,2,1,0:T(8,128)(2,1)S(1)} copy-done((bf16[1,6,48,192]{3,2,1,0:T(8,128)(2,1)S(1)}, bf16[1,6,48,192]{3,2,1,0:T(8,128)(2,1)}, u32[]{:S(2)}) %copy-start.4) | copy-done | bytes 110616
  6.2 0.0 copy-start.5
  6.2 0.9 %copy-done.5 = bf16[192,144]{1,0:T(8,128)(2,1)S(1)} copy-done((bf16[192,144]{1,0:T(8,128)(2,1)S(1)}, bf16[192,144]{1,0:T(8,128)(2,1)}, u32[]{:S(2)}) %copy-start.5) | copy-done | bytes 55320
  7.1 0.0 copy-start.6
  7.1 0.9 %copy-done.6 = bf16[2,192,12]{2,1,0:T(8,128)(2,1)S(1)} copy-done((bf16[2,192,12]{2,1,0:T(8,128)(2,1)S(1)}, bf16[2,192,12]{2,1,0:T(8,128)(2,1)}, u32[]{:S(2)}) %copy-start.6) | copy-done | bytes 9240
  8.0 0.0 copy-start.7
  8.0 0.9 %copy-done.7 = bf16[144,192]{1,0:T(8,128)(2,1)S(1)} copy-done((bf16[144,192]{1,0:T(8,128)(2,1)S(1)}, bf16[144,192]{1,0:T(8,128)(2,1)}, u32[]{:S(2)}) %copy-start.7) | copy-done | bytes 55320
  8.9 0.0 copy-start.9
  8.9 0.8 %copy-done.9 = bf16[144,72]{1,0:T(8,128)(2,1)S(1)} copy-done((bf16[144,72]{1,0:T(8,128)(2,1)S(1)}, bf16[144,72]{1,0:T(8,128)(2,1)}, u32[]{:S(2)}) %copy-start.9) | copy-done | bytes 20760
  9.7 0.0 copy-start.10
  9.7 0.7 %copy-done.10 = bf16[2,12,192]{2,1,0:T(8,128)(2,1)S(1)} copy-done((bf16[2,12,192]{2,1,0:T(8,128)(2,1)S(1)}, bf16[2,12,192]{2,1,0:T(8,128)(2,1)}, u32[]{:S(2)}) %copy-start.10) | copy-done | bytes 9240
  10.4 27.9 %shard_map.140 = (bf16[288,192]{1,0:T(8,128)(2,1)S(1)}, bf16[4,4,24,384]{3,2,1,0:T(8,128)(2,1)S(1)}) custom-call(bf16[288,192]{1,0:T(8,128)(2,1)S(1)} %bitcast.5, bf16[288,192]{1,0:T(8,128)(2,1)S(1)} %bitcast.6, bf16[144,384]{1,0:T(8,128)(2,1)S(1)} %reshape.24.refs_2_, bf16[72,12]{1,0:T(8,128)(2,1)S(1)} %bitcast.8, bf16[384,384]{1,0:T(8,128)(2,1)S(1)} %copy-done, ...), custom_call_target="tpu_custom_call" | custom-call | tf_op jit(solution)/shard_map/pallas_call | solution.py:289
  38.2 0.9 %convert_multiply_fusion = f32[4,4,24,384]{3,2,1,0:T(8,128)} fusion(bf16[4,4,24,384]{3,2,1,0:T(8,128)(2,1)S(1)} %get-tuple-element.5), kind=kLoop, calls=%fused_computation | loop fusion | flops 294912 | bytes 884736 | tf_op jit(solution)/shard_map/mul | solution.py:331
  39.1 0.7 %copy.17 = bf16[1,6,48,192]{3,2,1,0:T(8,128)(2,1)} copy(bf16[1,6,48,192]{3,2,1,0:T(8,128)(2,1)S(1)} %bitcast.7) | data formatting | bytes 221184
Async XLA Ops:
  0.6 1.8 %copy-start.2 = (bf16[288,384]{1,0:T(8,128)(2,1)S(1)}, bf16[288,384]{1,0:T(8,128)(2,1)}, u32[]{:S(2)}) copy-start(bf16[288,384]{1,0:T(8,128)(2,1)} %constant.19.clone.refs_6_) | copy-start | bytes 663556
  1.5 1.0 %copy-start.8 = (bf16[72,144]{1,0:T(8,128)(2,1)S(1)}, bf16[72,144]{1,0:T(8,128)(2,1)}, u32[]{:S(2)}) copy-start(bf16[72,144]{1,0:T(8,128)(2,1)} %constant.23.clone.refs_10_) | copy-start | bytes 62212
  2.5 1.0 %copy-start = (bf16[384,384]{1,0:T(8,128)(2,1)S(1)}, bf16[384,384]{1,0:T(8,128)(2,1)}, u32[]{:S(2)}) copy-start(bf16[384,384]{1,0:T(8,128)(2,1)} %refs_4_.1) | copy-start | bytes 884740
  3.4 1.0 %copy-start.1 = (bf16[384,288]{1,0:T(8,128)(2,1)S(1)}, bf16[384,288]{1,0:T(8,128)(2,1)}, u32[]{:S(2)}) copy-start(bf16[384,288]{1,0:T(8,128)(2,1)} %constant.18.clone.refs_5_) | copy-start | bytes 663556
  4.4 0.9 %copy-start.3 = (bf16[1,6,48,192]{3,2,1,0:T(8,128)(2,1)S(1)}, bf16[1,6,48,192]{3,2,1,0:T(8,128)(2,1)}, u32[]{:S(2)}) copy-start(bf16[1,6,48,192]{3,2,1,0:T(8,128)(2,1)} %param.13) | copy-start | bytes 331780
  5.3 0.9 %copy-start.4 = (bf16[1,6,48,192]{3,2,1,0:T(8,128)(2,1)S(1)}, bf16[1,6,48,192]{3,2,1,0:T(8,128)(2,1)}, u32[]{:S(2)}) copy-start(bf16[1,6,48,192]{3,2,1,0:T(8,128)(2,1)} %param.14) | copy-start | bytes 331780
  6.2 0.9 %copy-start.5 = (bf16[192,144]{1,0:T(8,128)(2,1)S(1)}, bf16[192,144]{1,0:T(8,128)(2,1)}, u32[]{:S(2)}) copy-start(bf16[192,144]{1,0:T(8,128)(2,1)} %constant.25.clone.refs_12_) | copy-start | bytes 165892
  7.1 0.9 %copy-start.6 = (bf16[2,192,12]{2,1,0:T(8,128)(2,1)S(1)}, bf16[2,192,12]{2,1,0:T(8,128)(2,1)}, u32[]{:S(2)}) copy-start(bf16[2,192,12]{2,1,0:T(8,128)(2,1)} %constant.21.clone.refs_8_) | copy-start | bytes 27652
  8.0 0.9 %copy-start.7 = (bf16[144,192]{1,0:T(8,128)(2,1)S(1)}, bf16[144,192]{1,0:T(8,128)(2,1)}, u32[]{:S(2)}) copy-start(bf16[144,192]{1,0:T(8,128)(2,1)} %constant.24.clone.refs_11_) | copy-start | bytes 165892
  8.9 0.8 %copy-start.9 = (bf16[144,72]{1,0:T(8,128)(2,1)S(1)}, bf16[144,72]{1,0:T(8,128)(2,1)}, u32[]{:S(2)}) copy-start(bf16[144,72]{1,0:T(8,128)(2,1)} %constant.22.clone.refs_9_) | copy-start | bytes 62212
  9.7 0.7 %copy-start.10 = (bf16[2,12,192]{2,1,0:T(8,128)(2,1)S(1)}, bf16[2,12,192]{2,1,0:T(8,128)(2,1)}, u32[]{:S(2)}) copy-start(bf16[2,12,192]{2,1,0:T(8,128)(2,1)} %constant.20.clone.refs_7_) | copy-start | bytes 27652

commit v2 on v1

--- a/solution.py
+++ b/solution.py
@@ -129,11 +129,14 @@
 
 def fused_kernel(
     lats, chans, members,
+    grad_hbm, pre_hbm, coeffs_hbm, leg_hbm, mix_hbm,
+    fwd_hbm, inv_hbm, sel_hbm, selt_hbm, spread_hbm, spreadt_hbm, mask_hbm, maskt_hbm,
+    out_hbm, full_hbm,
+    out_ref, full_ref,
     grad_ref, pre_ref, coeffs_ref, leg_ref, mix_ref,
     fwd_ref, inv_ref, sel_ref, selt_ref, spread_ref, spreadt_ref, mask_ref, maskt_ref,
-    out_ref, full_ref,
-    lbuf, sbuf, rbuf, sbuf2, rbuf2, wown, w1s, w1r, w2own, w2s, w2r,
-    lsem, esem, fsem, r1sem, r2sem, g1sem, g2sem,
+    stored, lbuf, sbuf, rbuf, sbuf2, rbuf2, wown, w1s, w1r, w2own, w2s, w2r,
+    isem, osem, lsem, esem, fsem, r1sem, r2sem, g1sem, g2sem,
 ):
     z, c, x = lax.axis_index("lat"), lax.axis_index("chan"), lax.axis_index("ens")
     owners, quads = lats * chans, members * chans
@@ -148,6 +151,20 @@
         q = lax.rem(quad + p, quads)
         return q, q // chans, lax.rem(q, chans)
 
+    sources = (
+        pre_hbm, grad_hbm, fwd_hbm, leg_hbm, sel_hbm, selt_hbm, spread_hbm, spreadt_hbm,
+        mask_hbm, maskt_hbm, coeffs_hbm, mix_hbm, inv_hbm,
+    )
+    targets = (
+        pre_ref, grad_ref, fwd_ref, leg_ref, sel_ref, selt_ref, spread_ref, spreadt_ref,
+        mask_ref, maskt_ref, coeffs_ref, mix_ref, inv_ref,
+    )
+    loads = [
+        pltpu.make_async_copy(source, target, isem.at[i])
+        for i, (source, target) in enumerate(zip(sources, targets))
+    ]
+    for load in loads:
+        load.start()
     barrier = pltpu.get_barrier_semaphore()
     for p in range(1, owners):
         _, pz, pc = owner_peer(p)
@@ -157,6 +174,8 @@
             target = {"ens": lax.rem(x + p, members), "chan": pc}
             pl.semaphore_signal(barrier, inc=1, device_id=target, device_id_type=MESH)
 
+    for load in loads[:3]:
+        load.wait()
     values = pre_ref[...].astype(F32)
     gate = jax.nn.sigmoid(values)
     scaled = (grad_ref[...].astype(F32) * gate * (1.0 + values * (1.0 - gate))).astype(BF16)
@@ -180,25 +199,35 @@
         copy = remote(sbuf.at[q], rbuf.at[c, z], pair(esem, p - 1), {"lat": pz, "chan": pc})
         copy.start()
         first.append(copy)
+    for load in loads[3:]:
+        load.wait()
     legs = remote(leg_ref, lbuf, pair(lsem, 0), {"ens": lax.rem(x + 1, members)})
     legs.start()
     started += first + [legs]
     rbuf[c, z] = sbuf[me]
     legs.wait_recv()
     other = lax.rem(x + 1, members)
-    mine, theirs = leg_ref[...], lbuf[...]
-    by_lat = dot(mine, sel_ref[x]) + dot(theirs, sel_ref[other])
-    analysis = (dot(spread_ref[...], by_lat.astype(BF16)) * mask_ref[...].astype(F32)).astype(BF16)
+    modes, degrees = leg_ref.shape[0], leg_ref.shape[2]
+    by_lat, synthesis = [], 0.0
+    for m in range(modes):
+        mine, theirs = leg_ref[m], lbuf[m]
+        down = ((0,), (0,))
+        by_lat.append(dot(mine, sel_ref[x], down) + dot(theirs, sel_ref[other], down))
+        by_row = dot(selt_ref[x], mine) + dot(selt_ref[other], theirs)
+        rows = spreadt_ref[m * degrees:(m + 1) * degrees, :]
+        synthesis = synthesis + dot(by_row.astype(BF16), rows)
+    by_lat = jnp.concatenate(by_lat, axis=0).astype(BF16)
+    analysis = (dot(spread_ref[...], by_lat) * mask_ref[...].astype(F32)).astype(BF16)
+    synthesis = (synthesis * maskt_ref[...].astype(F32)).astype(BF16)
     across = ((1,), (1,))
-    by_row = dot(selt_ref[x], mine, across) + dot(selt_ref[other], theirs, across)
-    synthesis = (dot(by_row.astype(BF16), spreadt_ref[...]) * maskt_ref[...].astype(F32)).astype(BF16)
+    stored[...] = coeffs_ref[...].reshape(stored.shape)
 
     for copy in first:
         copy.wait_recv()
     halves = [dot(analysis, rbuf[h].reshape(lats * pad, cols)) for h in range(chans)]
     coef = jnp.concatenate(halves, axis=1).astype(BF16)
 
-    weight = dot(coeffs_ref[...], coef, ((0,), (0,))).reshape(w1s.shape)
+    weight = dot(stored[...], coef, ((0,), (0,))).reshape(w1s.shape)
     wown[...] = weight
     w1s[...] = weight.astype(BF16)
     reduce1 = []
@@ -240,6 +269,8 @@
         copy.wait_recv()
     spatial = dot(inv_ref[...], rbuf2[...].reshape(owners * pad, cols))
     out_ref[...] = (grad_ref[...].astype(F32) + spatial).astype(BF16)
+    stores = [pltpu.make_async_copy(out_ref, out_hbm, osem.at[0])]
+    stores[0].start()
 
     piece = w2own[z]
     for p, copy in enumerate(reduce2):
@@ -266,9 +297,13 @@
             gather2.append(copy)
     for copy in gather2:
         copy.wait_recv()
+    stores.append(pltpu.make_async_copy(full_ref, full_hbm, osem.at[1]))
+    stores[1].start()
     started += gather2
     for copy in started:
         copy.wait_send()
+    for store in stores:
+        store.wait()
 
 
 def fused(grad_out, pre_act, coeffs, legendre, mixing):
@@ -281,21 +316,32 @@
     part, piece = channels // quads, channels // quads // lats
     constants = tables(rows, lon, lats, chans, members, modes, degrees)
     dma = pltpu.SemaphoreType.DMA
-    vmem = pl.BlockSpec(memory_space=pltpu.VMEM)
 
     def kernel(*refs):
         fused_kernel(lats, chans, members, *refs)
 
+    operands = (
+        grad_out.reshape(rows * lon, cols),
+        pre_act.reshape(rows * lon, cols),
+        coeffs.reshape(modes * degrees, 2, channels),
+        legendre.transpose(0, 2, 1),
+        mixing,
+        *constants,
+    )
     result, weight = pl.pallas_call(
         kernel,
         out_shape=(
             jax.ShapeDtypeStruct((rows * lon, cols), BF16),
             jax.ShapeDtypeStruct((quads, lats, piece, channels), BF16),
         ),
-        in_specs=[vmem] * 13,
-        out_specs=(vmem, vmem),
+        in_specs=[pl.BlockSpec(memory_space=pltpu.HBM)] * 13,
+        out_specs=(pl.BlockSpec(memory_space=pltpu.HBM),) * 2,
         scratch_shapes=[
-            pltpu.VMEM((modes * degrees, held), BF16),
+            pltpu.VMEM((rows * lon, cols), BF16),
+            pltpu.VMEM((quads, lats, piece, channels), BF16),
+            *[pltpu.VMEM(operand.shape, BF16) for operand in operands],
+            pltpu.VMEM((modes * degrees * 2, channels), BF16),
+            pltpu.VMEM((modes, held, degrees), BF16),
             pltpu.VMEM((owners, pad, cols), BF16),
             pltpu.VMEM((chans, lats, pad, cols), BF16),
             pltpu.VMEM((chans, lats, pad, cols), BF16),
@@ -306,6 +352,8 @@
             pltpu.VMEM((lats, piece, channels), F32),
             pltpu.VMEM((lats, piece, channels), BF16),
             pltpu.VMEM((lats - 1, piece, channels), BF16),
+            dma((len(operands),)),
+            dma((2,)),
             dma((2, 1)),
             dma((2, owners - 1)),
             dma((2, owners - 1)),
@@ -315,16 +363,9 @@
             dma((2, quads - 1, lats)),
         ],
         compiler_params=pltpu.CompilerParams(
-            collective_id=0, has_side_effects=True, vmem_limit_bytes=32 << 20
+            collective_id=0, has_side_effects=True, vmem_limit_bytes=60 << 20
         ),
-    )(
-        grad_out.reshape(rows * lon, cols),
-        pre_act.reshape(rows * lon, cols),
-        coeffs.reshape(modes * degrees * 2, channels),
-        legendre.reshape(modes * degrees, held),
-        mixing,
-        *constants,
-    )
+    )(*operands)
     scale = 1.0 / (members * lon // 2)
     return (
         result.reshape(grad_out.shape),

time: 40.3 us -> 32.2 us (0.80)
  local copies, waits for them, and re-layouts: 10.4 us -> 0.67 us
  Pallas kernels: 27.9 us -> 28.9 us
  other arithmetic: 0.87 us -> 1.86 us
    unnamed x24 -> x3, local copies, waits for them, and re-layouts: 9.41 us -> 0.67 us
    pallas_call x1, Pallas kernels: 27.9 us -> 28.9 us  [fused(): pl.pallas_call(kernel, out_shape=(jax.ShapeDtypeStruct((rows * lon, cols)...]
    mul x1, other arithmetic: 0.87 us -> 1.86 us  [fused(): weight.astype(F32).reshape(channels, channels) * scale]
    reshape x1 -> x0, local copies, waits for them, and re-layouts: 0.95 us -> none  [fused(): coeffs.reshape(modes * degrees * 2, channels)]
where the time goes in v2:
time: 32.2 us; the launch traced here: 32.1 us
  Pallas kernels  28.9 us (90%)
  other arithmetic  1.86 us (6%)
  local copies, waits for them, and re-layouts  0.67 us (2%)
  between operations  0.65 us (2%)
    pallas_call x1, Pallas kernels, fused(): pl.pallas_call(kernel, out_shape=(jax.ShapeDtypeStruct((rows * lon, cols)...  28.9 us
    mul x1, other arithmetic, fused(): weight.astype(F32).reshape(channels, channels) * scale  1.86 us
    unnamed x3, local copies, waits for them, and re-layouts  0.67 us

profile of v2, /device:TPU:0, one launch (start us, length us, event | category | flops | bytes accessed | tf_op | source)
XLA Modules:
  0.0 32.1 jit_solution(6676340767407572869)
XLA Ops:
  0.6 28.9 %shard_map.140 = (bf16[288,192]{1,0:T(8,128)(2,1)}, bf16[4,4,24,384]{3,2,1,0:T(8,128)(2,1)}) custom-call(bf16[288,192]{1,0:T(8,128)(2,1)} %bitcast.7, bf16[288,192]{1,0:T(8,128)(2,1)} %bitcast.8, bf16[72,2,384]{2,1,0:T(2,128)(2,1)} %bitcast.10, bf16[3,12,24]{2,1,0:T(8,128)(2,1)} %bitcast.11, bf16[384,384]{1,0:T(8,128)(2,1)} %refs_4_.1, ...), custom_call_target="tpu_custom_call" | custom-call | tf_op jit(solution)/shard_map/pallas_call | solution.py:331
  29.5 0.0 copy-start
  29.5 1.9 %convert_multiply_fusion = f32[4,4,24,384]{3,2,1,0:T(8,128)} fusion(bf16[4,4,24,384]{3,2,1,0:T(8,128)(2,1)} %get-tuple-element.5), kind=kLoop, calls=%fused_computation | loop fusion | flops 294912 | bytes 884736 | tf_op jit(solution)/shard_map/mul | solution.py:372
  31.4 0.0 copy-done
  31.4 0.7 %copy.16 = bf16[1,6,48,192]{3,2,1,0:T(8,128)(2,1)} copy(bf16[1,6,48,192]{3,2,1,0:T(8,128)(2,1)S(1)} %bitcast.9) | data formatting | bytes 221184
Async XLA Ops:
  29.5 1.9 %copy-start = (bf16[288,192]{1,0:T(8,128)(2,1)S(1)}, bf16[288,192]{1,0:T(8,128)(2,1)}, u32[]{:S(2)}) copy-start(bf16[288,192]{1,0:T(8,128)(2,1)} %get-tuple-element.4) | copy-start | bytes 331780

commit v3 on v2

--- a/solution.py
+++ b/solution.py
@@ -91,27 +91,44 @@
     return lax.dot_general(a, b, (dims, ((), ())), preferred_element_type=F32)
 
 
+LANES = 128
+
+
+def slots(rows, width):
+    whole = [(a, a, k) for a in range(rows) for k in range(width)]
+    paired = [(a, a + 1, k) for a in range(0, rows, 2) for k in range(width)]
+    return whole, paired
+
+
+def padded(rows, width):
+    return -(-(rows + rows // 2) * width // 16) * 16
+
+
 def tables(rows, lon, lats, chans, members, modes, degrees):
     owners = lats * chans
     width = 2 * modes
-    pad = -(-rows * width // 16) * 16
+    pad = padded(rows, width)
     n = np.arange(lon)[:, None]
     m = np.arange(lon // 2)[None, :]
     angles = np.float32(2.0 * math.pi / lon) * (n * m % lon).astype(np.float32)
     table = np.stack([np.cos(angles), -np.sin(angles)], axis=2).reshape(lon, lon)
     table = (table * np.float32(math.sqrt(2.0 / lon))).astype(np.float32)
-    inverse = np.zeros((rows, lon, owners, pad), np.float32)
-    for a in range(rows):
+    groups = rows + rows // 2
+    inverse = np.zeros((groups, lon, owners, pad), np.float32)
+    for g in range(groups):
         for d in range(owners):
-            inverse[a, :, d, a * width:(a + 1) * width] = table[:, d * width:(d + 1) * width]
-    inverse = inverse.reshape(rows * lon, owners * pad)
-    lat_of = np.full((lats, pad), -1)
-    key_of = np.full((lats, pad), -1)
+            inverse[g, :, d, g * width:(g + 1) * width] = table[:, d * width:(d + 1) * width]
+    inverse = inverse.reshape(groups * lon, owners * pad)
+    whole, paired = slots(rows, width)
+    lat_of = np.full((3, lats, pad), -1)
+    key_of = np.full((3, lats, pad), -1)
     for z in range(lats):
-        for a in range(rows):
-            for k in range(width):
-                lat_of[z, a * width + k] = z * rows + a
-                key_of[z, a * width + k] = k
+        for i, (even, odd, k) in enumerate(whole + paired):
+            if i < len(whole):
+                lat_of[0, z, i], key_of[0, z, i] = z * rows + even, k
+            else:
+                lat_of[1, z, i], key_of[1, z, i] = z * rows + even, k
+                lat_of[2, z, i], key_of[2, z, i] = z * rows + odd, k
     lat_of, key_of = lat_of.reshape(-1), key_of.reshape(-1)
     held = rows * lats // members
     select = (lat_of[None, :] == np.arange(members * held)[:, None]).astype(np.float32)
@@ -128,11 +145,11 @@
 
 
 def fused_kernel(
-    lats, chans, members,
+    lats, chans, members, lon,
     grad_hbm, pre_hbm, coeffs_hbm, leg_hbm, mix_hbm,
     fwd_hbm, inv_hbm, sel_hbm, selt_hbm, spread_hbm, spreadt_hbm, mask_hbm, maskt_hbm,
     out_hbm, full_hbm,
-    out_ref, full_ref,
+    out_ref, full_ref, wide_ref,
     grad_ref, pre_ref, coeffs_ref, leg_ref, mix_ref,
     fwd_ref, inv_ref, sel_ref, selt_ref, spread_ref, spreadt_ref, mask_ref, maskt_ref,
     stored, lbuf, sbuf, rbuf, sbuf2, rbuf2, wown, w1s, w1r, w2own, w2s, w2r,
@@ -141,7 +158,7 @@
     z, c, x = lax.axis_index("lat"), lax.axis_index("chan"), lax.axis_index("ens")
     owners, quads = lats * chans, members * chans
     me, quad = z * chans + c, x * chans + c
-    pad, cols = rbuf.shape[2], rbuf.shape[3]
+    pad, cols, blocks = rbuf.shape[2], grad_ref.shape[1], lats * rbuf.shape[2]
 
     def owner_peer(p):
         q = lax.rem(me + p, owners)
@@ -178,8 +195,12 @@
         load.wait()
     values = pre_ref[...].astype(F32)
     gate = jax.nn.sigmoid(values)
-    scaled = (grad_ref[...].astype(F32) * gate * (1.0 + values * (1.0 - gate))).astype(BF16)
-    sbuf[...] = dot(fwd_ref[...], scaled).astype(BF16).reshape(owners, pad, cols)
+    scaled = grad_ref[...].astype(F32) * gate * (1.0 + values * (1.0 - gate))
+    points, half = scaled.shape[0], LANES // 2
+    tail = scaled[:, LANES:].reshape(-1, 2, lon, half)
+    paired = jnp.concatenate([tail[:, 0], tail[:, 1]], axis=-1).reshape(-1, LANES)
+    packed = jnp.concatenate([scaled[:, :LANES], paired], axis=0).astype(BF16)
+    sbuf[...] = dot(fwd_ref[...], packed).astype(BF16).reshape(owners, pad, LANES)
 
     pl.semaphore_wait(barrier, owners - 1 + (members - 1) * chans)
 
@@ -224,7 +245,11 @@
 
     for copy in first:
         copy.wait_recv()
-    halves = [dot(analysis, rbuf[h].reshape(lats * pad, cols)) for h in range(chans)]
+    halves = []
+    for h in range(chans):
+        held = rbuf[h].reshape(blocks, LANES)
+        wide, even, odd = (dot(analysis[:, v * blocks:(v + 1) * blocks], held) for v in range(3))
+        halves += [wide, even[:, :half] + odd[:, half:]]
     coef = jnp.concatenate(halves, axis=1).astype(BF16)
 
     weight = dot(stored[...], coef, ((0,), (0,))).reshape(w1s.shape)
@@ -239,8 +264,19 @@
     started += reduce1
 
     for h in range(chans):
-        mixed = dot(coef, mix_ref[h * cols:(h + 1) * cols, :], across).astype(BF16)
-        sbuf2[h] = dot(synthesis, mixed).astype(BF16).reshape(lats, pad, cols)
+        mixed = dot(coef, mix_ref[h * cols:(h + 1) * cols, :], across)
+        rest = mixed[:, LANES:]
+        none = jnp.zeros_like(rest)
+        sides = (
+            mixed[:, :LANES],
+            jnp.concatenate([rest, none], axis=1),
+            jnp.concatenate([none, rest], axis=1),
+        )
+        returned = sum(
+            dot(synthesis[v * blocks:(v + 1) * blocks], side.astype(BF16))
+            for v, side in enumerate(sides)
+        )
+        sbuf2[h] = returned.astype(BF16).reshape(lats, pad, LANES)
     second = []
     for p in range(1, owners):
         q, pz, pc = owner_peer(p)
@@ -267,7 +303,10 @@
 
     for copy in second:
         copy.wait_recv()
-    spatial = dot(inv_ref[...], rbuf2[...].reshape(owners * pad, cols))
+    spatial = dot(inv_ref[...], rbuf2[...].reshape(owners * pad, LANES))
+    pairs = spatial[points:].reshape(-1, 1, lon, LANES)
+    rest = jnp.concatenate([pairs[..., :half], pairs[..., half:]], axis=1).reshape(points, half)
+    spatial = jnp.concatenate([spatial[:points], rest], axis=1)
     out_ref[...] = (grad_ref[...].astype(F32) + spatial).astype(BF16)
     stores = [pltpu.make_async_copy(out_ref, out_hbm, osem.at[0])]
     stores[0].start()
@@ -295,15 +334,34 @@
             copy = remote(block, block, pair(g2sem, p - 1, s), {"ens": px, "chan": pc})
             copy.start()
             gather2.append(copy)
-    for copy in gather2:
-        copy.wait_recv()
-    stores.append(pltpu.make_async_copy(full_ref, full_hbm, osem.at[1]))
-    stores[1].start()
+    part = full_ref.shape[1] * full_ref.shape[2]
+    scale = 1.0 / (members * lon // 2)
+    for p in range(quads):
+        if p > 0:
+            for s in range(lats):
+                gather2[s * (quads - 1) + p - 1].wait_recv()
+        block = lax.rem(quad + quads - p, quads)
+        place = pl.ds(pl.multiple_of(block * part, part), part)
+        wide_ref[place, :] = full_ref[block].astype(F32).reshape(part, -1) * scale
+        store = pltpu.make_async_copy(wide_ref.at[place], full_hbm.at[place], osem.at[1 + p])
+        store.start()
+        stores.append(store)
     started += gather2
     for copy in started:
         copy.wait_send()
     for store in stores:
         store.wait()
+
+
+def copy_kernel(first_in, second_in, first_out, second_out, sem):
+    copies = (
+        pltpu.make_async_copy(second_in, second_out, sem.at[1]),
+        pltpu.make_async_copy(first_in, first_out, sem.at[0]),
+    )
+    for copy in copies:
+        copy.start()
+    for copy in copies:
+        copy.wait()
 
 
 def fused(grad_out, pre_act, coeffs, legendre, mixing):
@@ -312,13 +370,13 @@
     members = lax.axis_size("ens")
     modes, degrees, held = legendre.shape
     owners, quads, channels = lats * chans, members * chans, cols * chans
-    pad = -(-rows * 2 * modes // 16) * 16
+    pad = padded(rows, 2 * modes)
     part, piece = channels // quads, channels // quads // lats
     constants = tables(rows, lon, lats, chans, members, modes, degrees)
     dma = pltpu.SemaphoreType.DMA
 
     def kernel(*refs):
-        fused_kernel(lats, chans, members, *refs)
+        fused_kernel(lats, chans, members, lon, *refs)
 
     operands = (
         grad_out.reshape(rows * lon, cols),
@@ -332,20 +390,21 @@
         kernel,
         out_shape=(
             jax.ShapeDtypeStruct((rows * lon, cols), BF16),
-            jax.ShapeDtypeStruct((quads, lats, piece, channels), BF16),
+            jax.ShapeDtypeStruct((channels, channels), F32),
         ),
         in_specs=[pl.BlockSpec(memory_space=pltpu.HBM)] * 13,
         out_specs=(pl.BlockSpec(memory_space=pltpu.HBM),) * 2,
         scratch_shapes=[
             pltpu.VMEM((rows * lon, cols), BF16),
             pltpu.VMEM((quads, lats, piece, channels), BF16),
+            pltpu.VMEM((channels, channels), F32),
             *[pltpu.VMEM(operand.shape, BF16) for operand in operands],
             pltpu.VMEM((modes * degrees * 2, channels), BF16),
             pltpu.VMEM((modes, held, degrees), BF16),
-            pltpu.VMEM((owners, pad, cols), BF16),
-            pltpu.VMEM((chans, lats, pad, cols), BF16),
-            pltpu.VMEM((chans, lats, pad, cols), BF16),
-            pltpu.VMEM((owners, pad, cols), BF16),
+            pltpu.VMEM((owners, pad, LANES), BF16),
+            pltpu.VMEM((chans, lats, pad, LANES), BF16),
+            pltpu.VMEM((chans, lats, pad, LANES), BF16),
+            pltpu.VMEM((owners, pad, LANES), BF16),
             pltpu.VMEM((quads, part, channels), F32),
             pltpu.VMEM((quads, part, channels), BF16),
             pltpu.VMEM((quads - 1, part, channels), BF16),
@@ -353,7 +412,7 @@
             pltpu.VMEM((lats, piece, channels), BF16),
             pltpu.VMEM((lats - 1, piece, channels), BF16),
             dma((len(operands),)),
-            dma((2,)),
+            dma((1 + quads,)),
             dma((2, 1)),
             dma((2, owners - 1)),
             dma((2, owners - 1)),
@@ -366,18 +425,27 @@
             collective_id=0, has_side_effects=True, vmem_limit_bytes=60 << 20
         ),
     )(*operands)
-    scale = 1.0 / (members * lon // 2)
-    return (
-        result.reshape(grad_out.shape),
-        weight.astype(F32).reshape(channels, channels) * scale,
-    )
+    result, weight = pl.pallas_call(
+        copy_kernel,
+        out_shape=(
+            jax.ShapeDtypeStruct(result.shape, BF16),
+            jax.ShapeDtypeStruct(weight.shape, F32),
+        ),
+        in_specs=[pl.BlockSpec(memory_space=pltpu.HBM)] * 2,
+        out_specs=(pl.BlockSpec(memory_space=pltpu.HBM),) * 2,
+        scratch_shapes=[dma((2,))],
+        compiler_params=pltpu.CompilerParams(vmem_limit_bytes=60 << 20),
+    )(result, weight)
+    return result.reshape(grad_out.shape), weight
 
 
 def fits(mesh, rows, lon, channels):
     lats, chans, members = (mesh.shape[axis] for axis in ("lat", "chan", "ens"))
     return (
         members == 2 and lats * chans <= 8 and rows * lon <= 512
-        and lon % 16 == 0 and channels % (members * chans * lats * 8) == 0
+        and lon % 16 == 0 and rows % 2 == 0
+        and channels // mesh.shape["chan"] == LANES + LANES // 2
+        and channels % (members * chans * lats * 8) == 0
     )
 
 

time: 32.2 us -> 51.4 us (1.60)
  Pallas kernels: 28.9 us -> 50.6 us
  other arithmetic: 1.86 us -> 0 us
  local copies, waits for them, and re-layouts: 0.67 us -> 0 us
    pallas_call x0 -> x1, Pallas kernels: none -> 23.5 us  [fused(): pl.pallas_call(copy_kernel, out_shape=(jax.ShapeDtypeStruct(result.shape,...]
    mul x1 -> x0, other arithmetic: 1.86 us -> none  [fused(): weight.astype(F32).reshape(channels, channels) * scale]
    pallas_call x1, Pallas kernels: 28.9 us -> 27.2 us  [fused(): pl.pallas_call(kernel, out_shape=(jax.ShapeDtypeStruct((rows * lon, cols)...]
    unnamed x3 -> x0, local copies, waits for them, and re-layouts: 0.67 us -> none
where the time goes in v3:
time: 51.4 us; the launch traced here: 51.2 us
  Pallas kernels  50.6 us (98%)
  between operations  0.64 us (1%)
    pallas_call x1, Pallas kernels, fused(): pl.pallas_call(kernel, out_shape=(jax.ShapeDtypeStruct((rows * lon, cols)...  27.2 us
    pallas_call x1, Pallas kernels, fused(): pl.pallas_call(copy_kernel, out_shape=(jax.ShapeDtypeStruct(result.shape,...  23.5 us

profile of v3, /device:TPU:0, one launch (start us, length us, event | category | flops | bytes accessed | tf_op | source)
XLA Modules:
  0.0 51.2 jit_solution(10800559893271785165)
XLA Ops:
  0.6 27.2 %shard_map.140 = (bf16[288,192]{1,0:T(8,128)(2,1)}, f32[384,384]{1,0:T(8,128)}) custom-call(bf16[288,192]{1,0:T(8,128)(2,1)} %bitcast.5, bf16[288,192]{1,0:T(8,128)(2,1)} %bitcast.6, bf16[72,2,384]{2,1,0:T(2,128)(2,1)} %bitcast.7, bf16[3,12,24]{2,1,0:T(8,128)(2,1)} %bitcast.8, bf16[384,384]{1,0:T(8,128)(2,1)} %refs_4_.1, ...), custom_call_target="tpu_custom_call" | custom-call | tf_op jit(solution)/shard_map/pallas_call | solution.py:389
  27.8 23.5 %shard_map.141 = (bf16[288,192]{1,0:T(8,128)(2,1)}, f32[384,384]{1,0:T(8,128)}) custom-call(bf16[288,192]{1,0:T(8,128)(2,1)} %get-tuple-element.6.first_in, f32[384,384]{1,0:T(8,128)} %get-tuple-element.7.second_in), custom_call_target="tpu_custom_call" | custom-call | tf_op jit(solution)/shard_map/pallas_call | solution.py:428

commit v4 on v3

--- a/solution.py
+++ b/solution.py
@@ -149,10 +149,10 @@
     grad_hbm, pre_hbm, coeffs_hbm, leg_hbm, mix_hbm,
     fwd_hbm, inv_hbm, sel_hbm, selt_hbm, spread_hbm, spreadt_hbm, mask_hbm, maskt_hbm,
     out_hbm, full_hbm,
-    out_ref, full_ref, wide_ref,
+    out_ref, full_ref,
     grad_ref, pre_ref, coeffs_ref, leg_ref, mix_ref,
     fwd_ref, inv_ref, sel_ref, selt_ref, spread_ref, spreadt_ref, mask_ref, maskt_ref,
-    stored, lbuf, sbuf, rbuf, sbuf2, rbuf2, wown, w1s, w1r, w2own, w2s, w2r,
+    stored, lbuf, sbuf, rbuf, sbuf2, rbuf2, w1s, w1r, w2own, w2s, w2r,
     isem, osem, lsem, esem, fsem, r1sem, r2sem, g1sem, g2sem,
 ):
     z, c, x = lax.axis_index("lat"), lax.axis_index("chan"), lax.axis_index("ens")
@@ -191,7 +191,7 @@
             target = {"ens": lax.rem(x + p, members), "chan": pc}
             pl.semaphore_signal(barrier, inc=1, device_id=target, device_id_type=MESH)
 
-    for load in loads[:3]:
+    for load in loads[:4]:
         load.wait()
     values = pre_ref[...].astype(F32)
     gate = jax.nn.sigmoid(values)
@@ -213,18 +213,18 @@
     def pair(sem, *index):
         return sem.at[(0,) + index], sem.at[(1,) + index]
 
-    started = []
+    legs = remote(leg_ref, lbuf, pair(lsem, 0), {"ens": lax.rem(x + 1, members)})
+    legs.start()
+    started = [legs]
     first = []
     for p in range(1, owners):
         q, pz, pc = owner_peer(p)
         copy = remote(sbuf.at[q], rbuf.at[c, z], pair(esem, p - 1), {"lat": pz, "chan": pc})
         copy.start()
         first.append(copy)
-    for load in loads[3:]:
+    started += first
+    for load in loads[4:]:
         load.wait()
-    legs = remote(leg_ref, lbuf, pair(lsem, 0), {"ens": lax.rem(x + 1, members)})
-    legs.start()
-    started += first + [legs]
     rbuf[c, z] = sbuf[me]
     legs.wait_recv()
     other = lax.rem(x + 1, members)
@@ -241,7 +241,8 @@
     analysis = (dot(spread_ref[...], by_lat) * mask_ref[...].astype(F32)).astype(BF16)
     synthesis = (synthesis * maskt_ref[...].astype(F32)).astype(BF16)
     across = ((1,), (1,))
-    stored[...] = coeffs_ref[...].reshape(stored.shape)
+    flat = coeffs_ref[...].reshape(stored.shape[::-1])
+    stored[...] = flat.astype(F32).T.astype(BF16)
 
     for copy in first:
         copy.wait_recv()
@@ -252,16 +253,20 @@
         halves += [wide, even[:, :half] + odd[:, half:]]
     coef = jnp.concatenate(halves, axis=1).astype(BF16)
 
-    weight = dot(stored[...], coef, ((0,), (0,))).reshape(w1s.shape)
-    wown[...] = weight
-    w1s[...] = weight.astype(BF16)
+    part = w1s.shape[1]
+
+    def weight(q):
+        return dot(stored[pl.ds(pl.multiple_of(q * part, part), part), :], coef)
+
     reduce1 = []
-    for p in range(1, quads):
+    for p in range(quads - 1, 0, -1):
         q, px, pc = quad_peer(p)
+        w1s[q] = weight(q).astype(BF16)
         copy = remote(w1s.at[q], w1r.at[p - 1], pair(r1sem, p - 1), {"ens": px, "chan": pc})
         copy.start()
         reduce1.append(copy)
     started += reduce1
+    own = weight(quad)
 
     for h in range(chans):
         mixed = dot(coef, mix_ref[h * cols:(h + 1) * cols, :], across)
@@ -286,10 +291,10 @@
     started += second
     rbuf2[me] = sbuf2[c, z]
 
-    total = wown[quad]
-    for p, copy in enumerate(reduce1):
+    total = own
+    for p, copy in zip(range(quads - 1, 0, -1), reduce1):
         copy.wait_recv()
-        total = total + w1r[p].astype(F32)
+        total = total + w1r[p - 1].astype(F32)
     total = total.reshape(w2own.shape)
     w2own[...] = total
     w2s[...] = total.astype(BF16)
@@ -334,16 +339,12 @@
             copy = remote(block, block, pair(g2sem, p - 1, s), {"ens": px, "chan": pc})
             copy.start()
             gather2.append(copy)
-    part = full_ref.shape[1] * full_ref.shape[2]
-    scale = 1.0 / (members * lon // 2)
     for p in range(quads):
         if p > 0:
             for s in range(lats):
                 gather2[s * (quads - 1) + p - 1].wait_recv()
         block = lax.rem(quad + quads - p, quads)
-        place = pl.ds(pl.multiple_of(block * part, part), part)
-        wide_ref[place, :] = full_ref[block].astype(F32).reshape(part, -1) * scale
-        store = pltpu.make_async_copy(wide_ref.at[place], full_hbm.at[place], osem.at[1 + p])
+        store = pltpu.make_async_copy(full_ref.at[block], full_hbm.at[block], osem.at[1 + p])
         store.start()
         stores.append(store)
     started += gather2
@@ -351,17 +352,6 @@
         copy.wait_send()
     for store in stores:
         store.wait()
-
-
-def copy_kernel(first_in, second_in, first_out, second_out, sem):
-    copies = (
-        pltpu.make_async_copy(second_in, second_out, sem.at[1]),
-        pltpu.make_async_copy(first_in, first_out, sem.at[0]),
-    )
-    for copy in copies:
-        copy.start()
-    for copy in copies:
-        copy.wait()
 
 
 def fused(grad_out, pre_act, coeffs, legendre, mixing):
@@ -390,22 +380,20 @@
         kernel,
         out_shape=(
             jax.ShapeDtypeStruct((rows * lon, cols), BF16),
-            jax.ShapeDtypeStruct((channels, channels), F32),
+            jax.ShapeDtypeStruct((quads, lats, piece, channels), BF16),
         ),
         in_specs=[pl.BlockSpec(memory_space=pltpu.HBM)] * 13,
         out_specs=(pl.BlockSpec(memory_space=pltpu.HBM),) * 2,
         scratch_shapes=[
             pltpu.VMEM((rows * lon, cols), BF16),
             pltpu.VMEM((quads, lats, piece, channels), BF16),
-            pltpu.VMEM((channels, channels), F32),
             *[pltpu.VMEM(operand.shape, BF16) for operand in operands],
-            pltpu.VMEM((modes * degrees * 2, channels), BF16),
+            pltpu.VMEM((channels, modes * degrees * 2), BF16),
             pltpu.VMEM((modes, held, degrees), BF16),
             pltpu.VMEM((owners, pad, LANES), BF16),
             pltpu.VMEM((chans, lats, pad, LANES), BF16),
             pltpu.VMEM((chans, lats, pad, LANES), BF16),
             pltpu.VMEM((owners, pad, LANES), BF16),
-            pltpu.VMEM((quads, part, channels), F32),
             pltpu.VMEM((quads, part, channels), BF16),
             pltpu.VMEM((quads - 1, part, channels), BF16),
             pltpu.VMEM((lats, piece, channels), F32),
@@ -425,17 +413,7 @@
             collective_id=0, has_side_effects=True, vmem_limit_bytes=60 << 20
         ),
     )(*operands)
-    result, weight = pl.pallas_call(
-        copy_kernel,
-        out_shape=(
-            jax.ShapeDtypeStruct(result.shape, BF16),
-            jax.ShapeDtypeStruct(weight.shape, F32),
-        ),
-        in_specs=[pl.BlockSpec(memory_space=pltpu.HBM)] * 2,
-        out_specs=(pl.BlockSpec(memory_space=pltpu.HBM),) * 2,
-        scratch_shapes=[dma((2,))],
-        compiler_params=pltpu.CompilerParams(vmem_limit_bytes=60 << 20),
-    )(result, weight)
+    weight = weight.astype(F32).reshape(channels, channels) * (1.0 / (members * lon // 2))
     return result.reshape(grad_out.shape), weight
 
 

time: 51.4 us -> 30.9 us (0.60)
  Pallas kernels: 50.6 us -> 27.6 us
  other arithmetic: 0 us -> 1.86 us
  local copies, waits for them, and re-layouts: 0 us -> 0.67 us
    pallas_call x1 -> x0, Pallas kernels: 23.5 us -> none  [fused(): pl.pallas_call(copy_kernel, out_shape=(jax.ShapeDtypeStruct(result.shape,...]
    mul x0 -> x1, other arithmetic: none -> 1.86 us  [fused(): weight.astype(F32).reshape(channels, channels)]
    unnamed x0 -> x3, local copies, waits for them, and re-layouts: none -> 0.67 us
where the time goes in v4:
time: 30.9 us; the launch traced here: 30.7 us
  Pallas kernels  27.6 us (89%)
  other arithmetic  1.86 us (6%)
  local copies, waits for them, and re-layouts  0.67 us (2%)
  between operations  0.65 us (2%)
    pallas_call x1, Pallas kernels, fused(): pl.pallas_call(kernel, out_shape=(jax.ShapeDtypeStruct((rows * lon, cols)...  27.6 us
    mul x1, other arithmetic, fused(): weight.astype(F32).reshape(channels, channels)  1.86 us
    unnamed x3, local copies, waits for them, and re-layouts  0.67 us

profile of v4, /device:TPU:0, one launch (start us, length us, event | category | flops | bytes accessed | tf_op | source)
XLA Modules:
  0.0 30.7 jit_solution(10217770301384664367)
XLA Ops:
  0.6 27.6 %shard_map.140 = (bf16[288,192]{1,0:T(8,128)(2,1)}, bf16[4,4,24,384]{3,2,1,0:T(8,128)(2,1)}) custom-call(bf16[288,192]{1,0:T(8,128)(2,1)} %bitcast.7, bf16[288,192]{1,0:T(8,128)(2,1)} %bitcast.8, bf16[72,2,384]{2,1,0:T(2,128)(2,1)} %bitcast.10, bf16[3,12,24]{2,1,0:T(8,128)(2,1)} %bitcast.11, bf16[384,384]{1,0:T(8,128)(2,1)} %refs_4_.1, ...), custom_call_target="tpu_custom_call" | custom-call | tf_op jit(solution)/shard_map/pallas_call | solution.py:379
  28.2 0.0 copy-start
  28.2 1.9 %convert_multiply_fusion = f32[4,4,24,384]{3,2,1,0:T(8,128)} fusion(bf16[4,4,24,384]{3,2,1,0:T(8,128)(2,1)} %get-tuple-element.5), kind=kLoop, calls=%fused_computation | loop fusion | flops 294912 | bytes 884736 | tf_op jit(solution)/shard_map/mul | solution.py:416
  30.1 0.0 copy-done
  30.1 0.7 %copy.16 = bf16[1,6,48,192]{3,2,1,0:T(8,128)(2,1)} copy(bf16[1,6,48,192]{3,2,1,0:T(8,128)(2,1)S(1)} %bitcast.9) | data formatting | bytes 221184
Async XLA Ops:
  28.2 1.9 %copy-start = (bf16[288,192]{1,0:T(8,128)(2,1)S(1)}, bf16[288,192]{1,0:T(8,128)(2,1)}, u32[]{:S(2)}) copy-start(bf16[288,192]{1,0:T(8,128)(2,1)} %get-tuple-element.4) | copy-start | bytes 331780

commit v5 on v4

--- a/solution.py
+++ b/solution.py
@@ -217,7 +217,7 @@
     legs.start()
     started = [legs]
     first = []
-    for p in range(1, owners):
+    for p in sorted(range(1, owners), key=lambda p: abs(p - owners // 2)):
         q, pz, pc = owner_peer(p)
         copy = remote(sbuf.at[q], rbuf.at[c, z], pair(esem, p - 1), {"lat": pz, "chan": pc})
         copy.start()
@@ -283,7 +283,7 @@
         )
         sbuf2[h] = returned.astype(BF16).reshape(lats, pad, LANES)
     second = []
-    for p in range(1, owners):
+    for p in sorted(range(1, owners), key=lambda p: abs(p - owners // 2)):
         q, pz, pc = owner_peer(p)
         copy = remote(sbuf2.at[pc, pz], rbuf2.at[me], pair(fsem, p - 1), {"lat": pz, "chan": pc})
         copy.start()
@@ -306,15 +306,17 @@
         reduce2.append(copy)
     started += reduce2
 
-    for copy in second:
-        copy.wait_recv()
-    spatial = dot(inv_ref[...], rbuf2[...].reshape(owners * pad, LANES))
-    pairs = spatial[points:].reshape(-1, 1, lon, LANES)
-    rest = jnp.concatenate([pairs[..., :half], pairs[..., half:]], axis=1).reshape(points, half)
-    spatial = jnp.concatenate([spatial[:points], rest], axis=1)
-    out_ref[...] = (grad_ref[...].astype(F32) + spatial).astype(BF16)
-    stores = [pltpu.make_async_copy(out_ref, out_hbm, osem.at[0])]
-    stores[0].start()
+    def finish():
+        for copy in second:
+            copy.wait_recv()
+        spatial = dot(inv_ref[...], rbuf2[...].reshape(owners * pad, LANES))
+        pairs = spatial[points:].reshape(-1, 1, lon, LANES)
+        rest = jnp.concatenate([pairs[..., :half], pairs[..., half:]], axis=1).reshape(points, half)
+        spatial = jnp.concatenate([spatial[:points], rest], axis=1)
+        out_ref[...] = (grad_ref[...].astype(F32) + spatial).astype(BF16)
+        stores = [pltpu.make_async_copy(out_ref, out_hbm, osem.at[0])]
+        stores[0].start()
+        return stores
 
     piece = w2own[z]
     for p, copy in enumerate(reduce2):
@@ -330,6 +332,8 @@
     started += gather1
     gather2 = []
     for s in range(lats):
+        if s == 1:
+            stores = finish()
         if s > 0:
             gather1[s - 1].wait_recv()
         source = lax.rem(z + lats - s, lats)

time: 30.9 us -> 30.9 us (level)
  no operation moved by 1% of the time
where the time goes in v5:
time: 30.9 us; the launch traced here: 30.7 us
  Pallas kernels  27.6 us (89%)
  other arithmetic  1.86 us (6%)
  local copies, waits for them, and re-layouts  0.67 us (2%)
  between operations  0.65 us (2%)
    pallas_call x1, Pallas kernels, fused(): pl.pallas_call(kernel, out_shape=(jax.ShapeDtypeStruct((rows * lon, cols)...  27.6 us
    mul x1, other arithmetic, fused(): weight.astype(F32).reshape(channels, channels)  1.86 us
    unnamed x3, local copies, waits for them, and re-layouts  0.67 us

profile of v5, /device:TPU:0, one launch (start us, length us, event | category | flops | bytes accessed | tf_op | source)
XLA Modules:
  0.0 30.7 jit_solution(6877679042901332229)
XLA Ops:
  0.6 27.6 %shard_map.140 = (bf16[288,192]{1,0:T(8,128)(2,1)}, bf16[4,4,24,384]{3,2,1,0:T(8,128)(2,1)}) custom-call(bf16[288,192]{1,0:T(8,128)(2,1)} %bitcast.7, bf16[288,192]{1,0:T(8,128)(2,1)} %bitcast.8, bf16[72,2,384]{2,1,0:T(2,128)(2,1)} %bitcast.10, bf16[3,12,24]{2,1,0:T(8,128)(2,1)} %bitcast.11, bf16[384,384]{1,0:T(8,128)(2,1)} %refs_4_.1, ...), custom_call_target="tpu_custom_call" | custom-call | tf_op jit(solution)/shard_map/pallas_call | solution.py:383
  28.2 0.0 copy-start
  28.2 1.9 %convert_multiply_fusion = f32[4,4,24,384]{3,2,1,0:T(8,128)} fusion(bf16[4,4,24,384]{3,2,1,0:T(8,128)(2,1)} %get-tuple-element.5), kind=kLoop, calls=%fused_computation | loop fusion | flops 294912 | bytes 884736 | tf_op jit(solution)/shard_map/mul | solution.py:420
  30.1 0.0 copy-done
  30.1 0.7 %copy.16 = bf16[1,6,48,192]{3,2,1,0:T(8,128)(2,1)} copy(bf16[1,6,48,192]{3,2,1,0:T(8,128)(2,1)S(1)} %bitcast.9) | data formatting | bytes 221184
Async XLA Ops:
  28.2 1.9 %copy-start = (bf16[288,192]{1,0:T(8,128)(2,1)S(1)}, bf16[288,192]{1,0:T(8,128)(2,1)}, u32[]{:S(2)}) copy-start(bf16[288,192]{1,0:T(8,128)(2,1)} %get-tuple-element.4) | copy-start | bytes 331780

commit v6 on v5

--- a/solution.py
+++ b/solution.py
@@ -153,7 +153,7 @@
     grad_ref, pre_ref, coeffs_ref, leg_ref, mix_ref,
     fwd_ref, inv_ref, sel_ref, selt_ref, spread_ref, spreadt_ref, mask_ref, maskt_ref,
     stored, lbuf, sbuf, rbuf, sbuf2, rbuf2, w1s, w1r, w2own, w2s, w2r,
-    isem, osem, lsem, esem, fsem, r1sem, r2sem, g1sem, g2sem,
+    isem, osem, lsem, esem, fsem, r1sem, r2sem, gsem,
 ):
     z, c, x = lax.axis_index("lat"), lax.axis_index("chan"), lax.axis_index("ens")
     owners, quads = lats * chans, members * chans
@@ -183,14 +183,12 @@
     for load in loads:
         load.start()
     barrier = pltpu.get_barrier_semaphore()
-    for p in range(1, owners):
-        _, pz, pc = owner_peer(p)
-        pl.semaphore_signal(barrier, inc=1, device_id={"lat": pz, "chan": pc}, device_id_type=MESH)
-    for p in range(1, members):
-        for pc in range(chans):
-            target = {"ens": lax.rem(x + p, members), "chan": pc}
-            pl.semaphore_signal(barrier, inc=1, device_id=target, device_id_type=MESH)
-
+    for p in range(quads):
+        for r in range(lats):
+            if p + r > 0:
+                _, px, pc = quad_peer(p)
+                target = {"ens": px, "chan": pc, "lat": lax.rem(z + r, lats)}
+                pl.semaphore_signal(barrier, inc=1, device_id=target, device_id_type=MESH)
     for load in loads[:4]:
         load.wait()
     values = pre_ref[...].astype(F32)
@@ -202,7 +200,7 @@
     packed = jnp.concatenate([scaled[:, :LANES], paired], axis=0).astype(BF16)
     sbuf[...] = dot(fwd_ref[...], packed).astype(BF16).reshape(owners, pad, LANES)
 
-    pl.semaphore_wait(barrier, owners - 1 + (members - 1) * chans)
+    pl.semaphore_wait(barrier, quads * lats - 1)
 
     def remote(src, dst, sems, target):
         return pltpu.make_async_remote_copy(
@@ -323,35 +321,21 @@
         copy.wait_recv()
         piece = piece + w2r[p].astype(F32)
     full_ref[quad, z] = piece.astype(BF16)
-    gather1 = []
-    for p in range(1, lats):
-        pz = lax.rem(z + p, lats)
-        copy = remote(full_ref.at[quad, z], full_ref.at[quad, z], pair(g1sem, p - 1), {"lat": pz})
+    everyone = [(p, r) for p in range(quads) for r in range(lats) if p + r > 0]
+    gather = []
+    for i, (p, r) in enumerate(everyone):
+        _, px, pc = quad_peer(p)
+        block = full_ref.at[quad, z]
+        target = {"ens": px, "chan": pc, "lat": lax.rem(z + r, lats)}
+        copy = remote(block, block, pair(gsem, i), target)
         copy.start()
-        gather1.append(copy)
-    started += gather1
-    gather2 = []
-    for s in range(lats):
-        if s == 1:
-            stores = finish()
-        if s > 0:
-            gather1[s - 1].wait_recv()
-        source = lax.rem(z + lats - s, lats)
-        for p in range(1, quads):
-            q, px, pc = quad_peer(p)
-            block = full_ref.at[quad, source]
-            copy = remote(block, block, pair(g2sem, p - 1, s), {"ens": px, "chan": pc})
-            copy.start()
-            gather2.append(copy)
-    for p in range(quads):
-        if p > 0:
-            for s in range(lats):
-                gather2[s * (quads - 1) + p - 1].wait_recv()
-        block = lax.rem(quad + quads - p, quads)
-        store = pltpu.make_async_copy(full_ref.at[block], full_hbm.at[block], osem.at[1 + p])
-        store.start()
-        stores.append(store)
-    started += gather2
+        gather.append(copy)
+    started += gather
+    stores = finish()
+    for copy in gather:
+        copy.wait_recv()
+    stores.append(pltpu.make_async_copy(full_ref, full_hbm, osem.at[1]))
+    stores[1].start()
     for copy in started:
         copy.wait_send()
     for store in stores:
@@ -410,8 +394,7 @@
             dma((2, owners - 1)),
             dma((2, quads - 1)),
             dma((2, lats - 1)),
-            dma((2, lats - 1)),
-            dma((2, quads - 1, lats)),
+            dma((2, quads * lats - 1)),
         ],
         compiler_params=pltpu.CompilerParams(
             collective_id=0, has_side_effects=True, vmem_limit_bytes=60 << 20

time: 30.9 us -> 31.7 us (1.026)
  Pallas kernels: 27.6 us -> 28.4 us
    pallas_call x1, Pallas kernels: 27.6 us -> 28.4 us  [fused(): pl.pallas_call(kernel, out_shape=(jax.ShapeDtypeStruct((rows * lon, cols)...]
where the time goes in v6:
time: 31.7 us; the launch traced here: 31.6 us
  Pallas kernels  28.4 us (90%)
  other arithmetic  1.86 us (6%)
  local copies, waits for them, and re-layouts  0.67 us (2%)
  between operations  0.65 us (2%)
    pallas_call x1, Pallas kernels, fused(): pl.pallas_call(kernel, out_shape=(jax.ShapeDtypeStruct((rows * lon, cols)...  28.4 us
    mul x1, other arithmetic, fused(): weight.astype(F32).reshape(channels, channels)  1.86 us
    unnamed x3, local copies, waits for them, and re-layouts  0.67 us

profile of v6, /device:TPU:0, one launch (start us, length us, event | category | flops | bytes accessed | tf_op | source)
XLA Modules:
  0.0 31.6 jit_solution(3641995561953180372)
XLA Ops:
  0.6 28.4 %shard_map.140 = (bf16[288,192]{1,0:T(8,128)(2,1)}, bf16[4,4,24,384]{3,2,1,0:T(8,128)(2,1)}) custom-call(bf16[288,192]{1,0:T(8,128)(2,1)} %bitcast.7, bf16[288,192]{1,0:T(8,128)(2,1)} %bitcast.8, bf16[72,2,384]{2,1,0:T(2,128)(2,1)} %bitcast.10, bf16[3,12,24]{2,1,0:T(8,128)(2,1)} %bitcast.11, bf16[384,384]{1,0:T(8,128)(2,1)} %refs_4_.1, ...), custom_call_target="tpu_custom_call" | custom-call | tf_op jit(solution)/shard_map/pallas_call | solution.py:367
  29.0 0.0 copy-start
  29.1 1.9 %convert_multiply_fusion = f32[4,4,24,384]{3,2,1,0:T(8,128)} fusion(bf16[4,4,24,384]{3,2,1,0:T(8,128)(2,1)} %get-tuple-element.5), kind=kLoop, calls=%fused_computation | loop fusion | flops 294912 | bytes 884736 | tf_op jit(solution)/shard_map/mul | solution.py:403
  30.9 0.0 copy-done
  30.9 0.7 %copy.16 = bf16[1,6,48,192]{3,2,1,0:T(8,128)(2,1)} copy(bf16[1,6,48,192]{3,2,1,0:T(8,128)(2,1)S(1)} %bitcast.9) | data formatting | bytes 221184
Async XLA Ops:
  29.0 1.9 %copy-start = (bf16[288,192]{1,0:T(8,128)(2,1)S(1)}, bf16[288,192]{1,0:T(8,128)(2,1)}, u32[]{:S(2)}) copy-start(bf16[288,192]{1,0:T(8,128)(2,1)} %get-tuple-element.4) | copy-start | bytes 331780
